TPU v7x, 128 devices: a whole 4x4x4 slice. The times are simulated.
128 devices in a mesh: row: 16 (over x, z_hi, core), col: 8 (over z_lo, y).
Axes of the slice: x: 4, y: 4, z: 4 (z_hi: 2, z_lo: 2; z = z_hi * 2 + z_lo), core: 2. Of those that a mesh axis runs over, the one named last changes fastest.
Arguments:
- thin_line_values: float32 [2048, 65536], P('row', 'col'), may hold values from 0 to 65520, as said below
- occupied_patch_flags: int32 [16, 512], P('row', 'col'), may hold values 0 or 1
- leader_vertical_patch: int32 [2], replicated, may hold values from 0 to 511, as said below
- leader_square_lines: float32 [2, 128, 65536], P(None, 'row', 'col'), may hold values from 0 to 65520, as said below
- leader_square_reciprocals: float32 [2, 128, 128], replicated, may hold values from 0 to 65520, as said below
- remaining_destination_line: int32 [2048], P('row'), may hold values from 0 to 15, as said below
- leading_square_lines: float32 [512, 65536], P('row', 'col'), may hold values from 0 to 65520, as said below
- leading_square_reciprocal: float32 [512, 512], replicated, may hold values from 0 to 65520, as said below
Outputs:
- dense_grid: float32 [4096, 65536], P('row', 'col')
Inputs may be any that keep to these rules, and one draw needn't show every extreme that they name: `leader_vertical_patch`: distinct column tiles; the last column tile is among them. `remaining_destination_line`: among the rows of one index of row no value appears more than 16 times; one value, the same for every index of row, appears exactly 16 times in each. `thin_line_values`: Integers. `leader_square_lines`: Integers. `leader_square_reciprocals`: Integers. `leading_square_lines`: Integers. `leading_square_reciprocal`: Integers.
All inputs are finite; a program needn't handle non-finite values. No bound on the sum of `occupied_patch_flags` on one device may be relied on, other than what follows from the above.
Results may differ from a plain program's by a relative error of at most 0.0003.
Values sent between devices are 32-bit elements; how exact they have to be, the bound alone decides.
A program may use at most 256 MiB of HBM per device.

v0:
```python
import jax
import jax.numpy as jnp
from jax import lax
from jax.sharding import PartitionSpec as P

TILE = 128
PANEL = 512
NPIV = 2
MAX_PER_DEST = 16
modulus = 65521.0


def broadcast(block, axis, owner):
    block = jnp.where(lax.axis_index(axis) == owner, block, jnp.zeros_like(block))
    return lax.psum(block, axis)


def reduce_mod(values):
    quotient = jnp.floor(values / modulus)
    remain = values - quotient * modulus
    remain = jnp.where(remain < 0.0, remain + modulus, remain)
    return jnp.where(remain >= modulus, remain - modulus, remain)


def split_limbs(values):
    upper = jnp.floor(values / 256.0)
    return (upper.astype(jnp.bfloat16), (values - upper * 256.0).astype(jnp.bfloat16))


def mul_mod(left, right):
    left_hi, left_lo = split_limbs(left)
    right_hi, right_lo = split_limbs(right)
    total = jnp.zeros((left.shape[0], right.shape[1]), jnp.float32)
    for offset in range(0, left.shape[1], 128):
        a_hi = left_hi[:, offset : offset + 128]
        a_lo = left_lo[:, offset : offset + 128]
        b_hi = right_hi[offset : offset + 128]
        b_lo = right_lo[offset : offset + 128]
        high = jnp.dot(a_hi, b_hi, preferred_element_type=jnp.float32)
        cross = jnp.dot(a_hi, b_lo, preferred_element_type=jnp.float32) + jnp.dot(
            a_lo, b_hi, preferred_element_type=jnp.float32
        )
        low = jnp.dot(a_lo, b_lo, preferred_element_type=jnp.float32)
        part = reduce_mod(reduce_mod(cross) * 256.0) + reduce_mod(high) * 15.0 + reduce_mod(low)
        total = reduce_mod(total + part)
    return total


def share_multiplier(values, owner):
    return broadcast(values, "col", owner)


def dispatched_lines(chain_differential, remaining_destination_line):
    outbound_lines = lax.axis_size("row")
    indicator_matrix = (
        remaining_destination_line[:, None] == jnp.arange(outbound_lines, dtype=jnp.int32)[None, :]
    ).astype(jnp.int32)
    landing_order = jnp.sum((jnp.cumsum(indicator_matrix, axis=0) - 1) * indicator_matrix, axis=1)
    incoming_places = remaining_destination_line * MAX_PER_DEST + landing_order
    outgoing = (
        jnp.zeros((outbound_lines * MAX_PER_DEST, chain_differential.shape[1]), jnp.float32)
        .at[incoming_places]
        .set(chain_differential)
    )
    return lax.all_to_all(outgoing, "row", split_axis=0, concat_axis=0, tiled=True)


def panel_step(chain_differential, leading_square_lines, leading_square_reciprocal):
    panel_terms = mul_mod(chain_differential[:, :PANEL], leading_square_reciprocal)
    lower = broadcast(panel_terms, "col", 0)
    strip = lax.all_gather(leading_square_lines, "row", axis=0, tiled=True)
    update = mul_mod(lower, strip)
    return reduce_mod(chain_differential - update) / modulus


def local(
    thin_line_values,
    occupied_patch_flags,
    leader_vertical_patch,
    leader_square_lines,
    leader_square_reciprocals,
    remaining_destination_line,
    leading_square_lines,
    leading_square_reciprocal,
):
    rows_dev, width_dev = thin_line_values.shape
    tiles_dev = width_dev // TILE
    shaped = thin_line_values.reshape(rows_dev // TILE, TILE, tiles_dev, TILE)
    shaped = shaped * occupied_patch_flags.astype(jnp.float32)[:, None, :, None]
    eliminated_lines = shaped.reshape(rows_dev, width_dev)
    for pivot in range(NPIV):
        block_rows = lax.all_gather(leader_square_lines[pivot], "row", axis=0, tiled=True)
        column = leader_vertical_patch[pivot]
        owner = column // tiles_dev
        offset = column % tiles_dev * TILE
        tile_now, owner = (lax.dynamic_slice_in_dim(eliminated_lines, offset, TILE, 1), owner)
        factor = share_multiplier(mul_mod(tile_now, leader_square_reciprocals[pivot]), owner)
        eliminated_lines = reduce_mod(eliminated_lines - mul_mod(factor, block_rows))
    patchwise_arrangement = dispatched_lines(eliminated_lines, remaining_destination_line)
    return panel_step(patchwise_arrangement, leading_square_lines, leading_square_reciprocal)


def solution(mesh):
    return jax.shard_map(
        local,
        mesh=mesh,
        in_specs=(
            P("row", "col"),
            P("row", "col"),
            P(),
            P(None, "row", "col"),
            P(),
            P("row"),
            P("row", "col"),
            P(),
        ),
        out_specs=P("row", "col"),
        check_vma=False,
    )
```

profile of v0, /device:TPU:1, one launch (start us, length us, event | category | flops | bytes accessed | tf_op | source)
XLA Modules:
  0.0 635.3 jit_solution(7856029149557377119)
XLA Ops:
  7.4 1.4 fusion.224
  11.3 0.7 convert_bitcast_fusion
  12.1 2.6 broadcast_multiply_fusion
  15.0 1.7 copy-done.3
  16.9 1.7 fusion.121
  18.7 0.9 fusion.223
  19.7 0.5 all-gather.10.cloned.1.call-update
  23.2 66.9 %all-reduce.4.cloned.1.call-done = f32[128,128]{1,0:T(8,128)} async-done(((f32[128,128]{1,0:T(8,128)}), f32[128,128]{1,0:T(8,128)}) %all-reduce.4.cloned.1.call-update) | async-done | bytes 65552 | tf_op jit(solution)/shard_map/psum | solution.py:15
  90.1 3.3 fusion.167
  93.5 0.5 copy-done.1
  93.9 0.7 fusion.70
  94.6 0.8 fusion.169
  95.4 1.4 copy-done.4
  96.8 9.7 %compare_select_fusion.54 = f32[128,8192]{1,0:T(8,128)S(1)} fusion(f32[128,8192]{1,0:T(8,128)S(1)} %copy-done.4, f32[128,8192]{1,0:T(8,128)S(1)} %fusion.167, f32[128,8192]{1,0:T(8,128)S(1)} %fusion.70, f32[128,8192]{1,0:T(8,128)S(1)} %fusion.169, f32[1,128,8192]{2,1,0:T(8,128)S(1)} %copy-done.1, f32[128,128]{1,0:T(8,128)S(1)} %copy-done.7), kind=kOutput, calls=%fused_computation.58 | convolution fusion | flops 340869120 | bytes 25231360 | tf_op jit(solution)/shard_map/dot_general | solution.py:40
  107.0 1.6 copy-done.10
  108.6 0.9 fusion.125
  109.5 29.2 %all-gather.10.cloned.1.call-done = f32[1,128,8192]{2,1,0:T(8,128)} async-done(((f32[1,8,8192]{2,1,0:T(8,128)}), f32[1,128,8192]{2,1,0:T(8,128)}) %all-gather.10.cloned.1.call-update) | async-done | bytes 4194320 | tf_op jit(solution)/shard_map/all_gather | solution.py:92
  138.7 42.9 %all-reduce.6.cloned.1.call-done = f32[128,128]{1,0:T(8,128)} async-done(((f32[128,128]{1,0:T(8,128)}), f32[128,128]{1,0:T(8,128)}) %all-reduce.6.cloned.1.call-update) | async-done | bytes 65552 | tf_op jit(solution)/shard_map/psum | solution.py:15
  181.6 3.2 fusion.171
  184.8 0.3 copy-done
  185.1 0.7 fusion.67
  185.8 0.8 fusion.173
  186.6 1.4 copy-done.11
  188.0 9.4 %fusion.25 = f32[128,8192]{1,0:T(8,128)} fusion(f32[128,8192]{1,0:T(8,128)S(1)} %copy-done.11, f32[128,8192]{1,0:T(8,128)S(1)} %fusion.171, f32[128,8192]{1,0:T(8,128)S(1)} %fusion.67, f32[128,8192]{1,0:T(8,128)S(1)} %fusion.173, f32[1,128,8192]{2,1,0:T(8,128)S(1)} %copy-done, f32[128,128]{1,0:T(8,128)S(1)} %copy-done.8), kind=kOutput, calls=%fused_computation.100 | convolution fusion | flops 330383360 | bytes 25231360 | tf_op jit(solution)/shard_map/dot_general | solution.py:40
  197.4 9.7 %scatter_custom_fusion = f32[256,8192]{1,0:T(8,128)} fusion(s32[128]{0:T(128)S(1)} %compare_select_fusion.127, f32[128,8192]{1,0:T(8,128)} %fusion.25, f32[]{:T(128)} %constant.215.clone.1, f32[]{:T(128)} %constant.231.clone.1, f32[]{:T(128)} %constant.230.clone.1, f32[]{:T(128)} %constant.229.clone.1), kind=kCustom, calls=%fused_computation.101 | custom fusion | flops 10485760 | bytes 12585472 | tf_op jit(solution)/shard_map/scatter | solution.py:63
  207.1 12.2 %all-to-all-start = ((f32[16,16,8192]{2,1,0:T(8,128)}), f32[16,16,8192]{2,1,0:T(8,128)}, u32[]{:S(2)}, u32[]{:S(2)}) async-start(f32[16,16,8192]{2,1,0:T(8,128)} %bitcast.69), calls=%async_computation | async-start | bytes 16777216 | tf_op jit(solution)/shard_map/all_to_all | solution.py:65
  219.5 131.2 %all-to-all-done = f32[16,16,8192]{2,1,0:T(8,128)} async-done(((f32[16,16,8192]{2,1,0:T(8,128)}), f32[16,16,8192]{2,1,0:T(8,128)}, u32[]{:S(2)}, u32[]{:S(2)}) %all-to-all-start) | async-done | bytes 8388640 | tf_op jit(solution)/shard_map/all_to_all | solution.py:65
  350.8 1.1 subtract_convert_fusion.3
  352.1 0.2 fusion.107
  352.3 0.2 fusion.100
  352.5 0.2 fusion.111
  352.7 0.2 fusion.104
  352.9 0.2 fusion.97
  353.1 0.2 fusion.91
  353.4 0.2 fusion.95
  353.8 0.2 fusion.109
  354.0 0.2 fusion.116
  354.2 0.2 convolution_add_fusion.6
  354.4 0.2 convolution_add_fusion.7
  354.6 0.2 convolution_add_fusion.8
  354.9 0.2 convolution_add_fusion.9
  355.1 4.5 fusion.88
  359.7 0.5 all-gather.6.cloned.1.call-update
  360.2 71.5 %all-reduce.8.cloned.1.call-done = f32[256,512]{1,0:T(8,128)} async-done(((f32[256,512]{1,0:T(8,128)}), f32[256,512]{1,0:T(8,128)}) %all-reduce.8.cloned.1.call-update) | async-done | bytes 524304 | tf_op jit(solution)/shard_map/psum | solution.py:15
  431.7 1.1 subtract_convert_fusion.2
  432.9 48.8 %all-gather.6.cloned.1.call-done = f32[512,8192]{1,0:T(8,128)} async-done(((f32[32,8192]{1,0:T(8,128)}), f32[512,8192]{1,0:T(8,128)}) %all-gather.6.cloned.1.call-update) | async-done | bytes 16777232 | tf_op jit(solution)/shard_map/all_gather | solution.py:71
  481.6 7.9 %subtract_convert_fusion = (bf16[512,8192]{1,0:T(8,128)(2,1)S(1)}, bf16[512,8192]{1,0:T(8,128)(2,1)S(1)}) fusion(f32[512,8192]{1,0:T(8,128)} %all-gather.6.cloned.1.call-done), kind=kLoop, calls=%fused_computation.43 | loop fusion | flops 25165824 | bytes 33554432 | tf_op jit(solution)/shard_map/convert_element_type | solution.py:27
  489.5 4.5 fusion.62
  494.0 4.5 fusion.55
  498.4 4.5 fusion.48
  502.9 4.5 fusion.59
  507.4 4.5 fusion.52
  511.9 4.5 fusion.45
  516.3 4.6 fusion.39
  521.0 4.5 fusion.43
  525.4 4.5 fusion.50
  530.0 1.5 fusion.57
  531.5 1.2 fusion.64
  532.7 8.0 %convolution_add_fusion = f32[256,8192]{1,0:T(8,128)} fusion(f32[256,8192]{1,0:T(8,128)} %fusion.43, bf16[512,8192]{1,0:T(8,128)(2,1)S(1)} %get-tuple-element.6, bf16[256,512]{1,0:T(8,128)(2,1)S(1)} %get-tuple-element.11), kind=kOutput, calls=%fused_computation.70 | convolution fusion | flops 538968064 | bytes 18939904 | tf_op jit(solution)/shard_map/dot_general | solution.py:40
  540.7 8.1 %convolution_add_fusion.1 = f32[256,8192]{1,0:T(8,128)} fusion(f32[256,8192]{1,0:T(8,128)} %fusion.50, bf16[512,8192]{1,0:T(8,128)(2,1)S(1)} %get-tuple-element.6, bf16[256,512]{1,0:T(8,128)(2,1)S(1)} %get-tuple-element.11), kind=kOutput, calls=%fused_computation.71 | convolution fusion | flops 538968064 | bytes 18939904 | tf_op jit(solution)/shard_map/dot_general | solution.py:40
  548.9 4.5 convolution_add_fusion.2
  553.3 5.4 convolution_add_fusion.3
  558.7 0.8 copy-done.2
  559.5 68.0 %fusion.17 = f32[256,8192]{1,0:T(8,128)} fusion(f32[256,8192]{1,0:T(8,128)} %bitcast.9, f32[256,8192]{1,0:T(8,128)} %fusion.39, f32[256,8192]{1,0:T(8,128)} %convolution_add_fusion, f32[256,8192]{1,0:T(8,128)} %fusion.48, f32[256,8192]{1,0:T(8,128)} %fusion.45, f32[256,8192]{1,0:T(8,128)S(1)} %copy-done.2, f32[256,8192]{1,0:T(8,128)} %fusion.55, ...), kind=kOutput, calls=%fused_computation.92 | convolution fusion | flops 1021313024 | bytes 111214592 | tf_op jit(solution)/shard_map/dot_general | solution.py:43
  (44 shorter events, 2.2 us)
Async XLA Ops:
  7.4 82.8 %all-reduce.4.cloned.1.call-start = ((), (), s32[]{:S(2)}) async-start(), calls=%async_computation.1 | async-start | bytes 131072 | tf_op jit(solution)/shard_map/psum | solution.py:15
  12.1 2.7 copy-start.5
  12.1 6.6 %copy-start.9 = (f32[2,8,8192]{2,1,0:T(8,128)S(1)}, f32[2,8,8192]{2,1,0:T(8,128)}, u32[]{:S(2)}) copy-start(f32[2,8,8192]{2,1,0:T(8,128)} %param.11) | copy-start | bytes 1572868
  12.1 10.7 %copy-start.12 = (s32[128]{0:T(128)S(1)}, s32[128]{0:T(128)}, u32[]{:S(2)}) copy-start(s32[128]{0:T(128)} %param.13) | copy-start | bytes 1540
  14.7 2.0 copy-start.3
  18.6 71.5 %all-gather.8.cloned.1.call-start = ((), (), s32[]{:S(2)}) async-start(), calls=%async_computation.5 | async-start | bytes 4456448 | tf_op jit(solution)/shard_map/all_gather | solution.py:92
  19.6 119.1 %all-gather.10.cloned.1.call-start = ((), (), s32[]{:S(2)}) async-start(), calls=%async_computation.6 | async-start | bytes 4456448 | tf_op jit(solution)/shard_map/all_gather | solution.py:92
  20.2 161.4 %all-reduce.6.cloned.1.call-start = ((), (), s32[]{:S(2)}) async-start(), calls=%async_computation.2 | async-start | bytes 131072 | tf_op jit(solution)/shard_map/psum | solution.py:15
  90.1 3.3 copy-start.7
  90.1 3.8 copy-start.1
  94.6 2.2 copy-start.4
  106.6 2.0 copy-start.10
  181.6 3.5 copy-start
  181.6 3.5 copy-start.8
  185.8 2.2 copy-start.11
  207.1 12.2 %copy-start.6 = (f32[512,512]{1,0:T(8,128)S(1)}, f32[512,512]{1,0:T(8,128)}, u32[]{:S(2)}) copy-start(f32[512,512]{1,0:T(8,128)} %param.15) | copy-start | bytes 3145732
  207.1 143.7 %all-to-all-start = ((f32[16,16,8192]{2,1,0:T(8,128)}), f32[16,16,8192]{2,1,0:T(8,128)}, u32[]{:S(2)}, u32[]{:S(2)}) async-start(f32[16,16,8192]{2,1,0:T(8,128)} %bitcast.69), calls=%async_computation | async-start | bytes 16777216 | tf_op jit(solution)/shard_map/all_to_all | solution.py:65
  219.3 212.4 %all-reduce.8.cloned.1.call-start = ((), (), s32[]{:S(2)}) async-start(), calls=%async_computation.3 | async-start | bytes 1048576 | tf_op jit(solution)/shard_map/psum | solution.py:15
  359.6 122.0 %all-gather.6.cloned.1.call-start = ((), (), s32[]{:S(2)}) async-start(), calls=%async_computation.4 | async-start | bytes 17825792 | tf_op jit(solution)/shard_map/all_gather | solution.py:71
  553.3 6.2 copy-start.2
Sparse Core Ops, SparseCore 0:
  18.8 71.3 all-reduce.3
  109.6 71.9 all-reduce.5
  359.8 71.9 all-reduce.7
Sparse Core Ops, SparseCore 1:
  21.5 59.7 all-gather.7
  83.9 54.8 all-gather.9
  362.5 119.1 all-gather.5
where the time goes:
time: 645 us; the launch traced here: 635 us
  waiting for transfers between devices  392 us (61%)
  matrix products  177 us (27%)
  other arithmetic  23.8 us (4%)
  between operations  20.7 us (3%)
  starting transfers between devices  12.4 us (2%)
  local copies, waits for them, and re-layouts  9.99 us (2%)
    psum x3, waiting for transfers between devices, broadcast(): return lax.psum(block, axis)  181 us
    all_to_all x1, waiting for transfers between devices, dispatched_lines(): lax.all_to_all(outgoing, 'row', split_axis=0, concat_axis=0, tiled=True)  131 us
    dot_general x12, matrix products, mul_mod(): low = jnp.dot(a_lo, b_lo, preferred_element_type=jnp.float32)  93.3 us
    all_gather x1, waiting for transfers between devices, panel_step(): strip = lax.all_gather(leading_square_lines, 'row', axis=0, tiled=True)  48.8 us
    dot_general x12, matrix products, mul_mod(): jnp.dot(a_lo, b_hi, preferred_element_type=jnp.float32)  48.5 us
    all_gather x2, waiting for transfers between devices, local(): lax.all_gather(leader_square_lines[pivot], 'row', axis=0, tiled=True)  29.2 us
    dot_general x12, matrix products, mul_mod(): high = jnp.dot(a_hi, b_hi, preferred_element_type=jnp.float32)  20.5 us
    dot_general x12, matrix products, mul_mod(): jnp.dot(a_hi, b_lo, preferred_element_type=jnp.float32)  14.4 us
  transfers between devices with their start and end apart: 7, of which 6 were waited for; matrix products, arithmetic and copies ran while one was open for 3% of the time, Pallas kernels for 0%

commit v1 on v0

--- a/solution.py
+++ b/solution.py
@@ -89,7 +89,11 @@
     shaped = shaped * occupied_patch_flags.astype(jnp.float32)[:, None, :, None]
     eliminated_lines = shaped.reshape(rows_dev, width_dev)
     for pivot in range(NPIV):
-        block_rows = lax.all_gather(leader_square_lines[pivot], "row", axis=0, tiled=True)
+        block_2 = leader_square_lines[pivot]
+        count = lax.axis_size("row")
+        blocks = jnp.stack([block_2 for _ in range(count)])
+        blocks = lax.all_to_all(blocks, "row", split_axis=0, concat_axis=0)
+        block_rows = jnp.concatenate(blocks, axis=0)
         column = leader_vertical_patch[pivot]
         owner = column // tiles_dev
         offset = column % tiles_dev * TILE

time: 645 us -> 672 us (1.042)
  starting transfers between devices: 12.4 us -> 45.7 us
  waiting for transfers between devices: 392 us -> 379 us
  matrix products: 177 us -> 188 us
    all_to_all x0 -> x2, waiting for transfers between devices: none -> 58 us  [local(): blocks = lax.all_to_all(blocks, 'row', split_axis=0, concat_axis=0)]
    psum x3, waiting for transfers between devices: 181 us -> 141 us  [broadcast(): return lax.psum(block, axis)]
    all_gather x2 -> x0, waiting for transfers between devices: 29.2 us -> none  [local(): lax.all_gather(leader_square_lines[pivot], 'row', axis=0, tiled=True)]
    all_to_all x0 -> x2, starting transfers between devices: none -> 21.8 us  [local(): blocks = lax.all_to_all(blocks, 'row', split_axis=0, concat_axis=0)]
    all_to_all x1, starting transfers between devices: 12.2 us -> 23.7 us  [dispatched_lines(): lax.all_to_all(outgoing, 'row', split_axis=0, concat_axis=0, tiled=True)]
  transfers between devices with their start and end apart: 7 -> 7, of which waited for: 6 -> 7; matrix products, arithmetic and copies ran while one was open for 3% -> 5% of each run, Pallas kernels for 0% -> 0%
where the time goes in v1:
time: 672 us; the launch traced here: 667 us
  waiting for transfers between devices  379 us (56%)
  matrix products  188 us (28%)
  starting transfers between devices  45.7 us (7%)
  other arithmetic  22.9 us (3%)
  between operations  20.3 us (3%)
  local copies, waits for them, and re-layouts  11.1 us (2%)
    psum x3, waiting for transfers between devices, broadcast(): return lax.psum(block, axis)  141 us
    all_to_all x1, waiting for transfers between devices, dispatched_lines(): lax.all_to_all(outgoing, 'row', split_axis=0, concat_axis=0, tiled=True)  131 us
    dot_general x12, matrix products, mul_mod(): low = jnp.dot(a_lo, b_lo, preferred_element_type=jnp.float32)  93 us
    all_to_all x2, waiting for transfers between devices, local(): blocks = lax.all_to_all(blocks, 'row', split_axis=0, concat_axis=0)  58 us
    dot_general x12, matrix products, mul_mod(): jnp.dot(a_lo, b_hi, preferred_element_type=jnp.float32)  50.8 us
    all_gather x1, waiting for transfers between devices, panel_step(): strip = lax.all_gather(leading_square_lines, 'row', axis=0, tiled=True)  48.9 us
    dot_general x12, matrix products, mul_mod(): high = jnp.dot(a_hi, b_hi, preferred_element_type=jnp.float32)  25 us
    all_to_all x1, starting transfers between devices, dispatched_lines(): lax.all_to_all(outgoing, 'row', split_axis=0, concat_axis=0, tiled=True)  23.7 us
  transfers between devices with their start and end apart: 7, of which 7 were waited for; matrix products, arithmetic and copies ran while one was open for 5% of the time, Pallas kernels for 0%

profile of v1, /device:TPU:1, one launch (start us, length us, event | category | flops | bytes accessed | tf_op | source)
XLA Modules:
  0.0 666.9 jit_solution(5476502917689073230)
XLA Ops:
  7.4 1.1 slice_bitcast_fusion
  8.4 2.4 stack.6
  10.8 9.3 %all-to-all-start = ((f32[16,8,8192]{2,1,0:T(8,128)}), f32[16,8,8192]{2,1,0:T(8,128)}, u32[]{:S(2)}, u32[]{:S(2)}) async-start(f32[16,8,8192]{2,1,0:T(8,128)} %stack.6), calls=%async_computation | async-start | bytes 8388608 | tf_op jit(solution)/shard_map/all_to_all | solution.py:95
  20.1 0.6 fusion.223
  23.5 2.6 broadcast_multiply_fusion
  26.5 1.6 copy-done.1
  28.1 0.8 fusion.121
  32.0 41.7 %all-to-all-done = f32[16,8,8192]{2,1,0:T(8,128)} async-done(((f32[16,8,8192]{2,1,0:T(8,128)}), f32[16,8,8192]{2,1,0:T(8,128)}, u32[]{:S(2)}, u32[]{:S(2)}) %all-to-all-start) | async-done | bytes 4194336 | tf_op jit(solution)/shard_map/all_to_all | solution.py:95
  73.7 2.4 stack.7
  76.0 12.5 %all-to-all-start.1 = ((f32[16,8,8192]{2,1,0:T(8,128)}), f32[16,8,8192]{2,1,0:T(8,128)}, u32[]{:S(2)}, u32[]{:S(2)}) async-start(f32[16,8,8192]{2,1,0:T(8,128)} %stack.7), calls=%async_computation.1 | async-start | bytes 8388608 | tf_op jit(solution)/shard_map/all_to_all | solution.py:95
  88.6 12.5 %all-reduce.4.cloned.1.call-done = f32[128,128]{1,0:T(8,128)} async-done(((f32[128,128]{1,0:T(8,128)}), f32[128,128]{1,0:T(8,128)}) %all-reduce.4.cloned.1.call-update) | async-done | bytes 65552 | tf_op jit(solution)/shard_map/psum | solution.py:15
  101.1 3.1 fusion.167
  104.2 2.9 fusion.70
  107.1 3.1 fusion.169
  110.2 0.3 copy-done.2
  110.5 11.4 %compare_select_fusion.54 = f32[128,8192]{1,0:T(8,128)S(1)} fusion(f32[128,8192]{1,0:T(8,128)S(1)} %copy-done.2, f32[128,8192]{1,0:T(8,128)S(1)} %fusion.167, f32[128,8192]{1,0:T(8,128)S(1)} %fusion.70, f32[128,8192]{1,0:T(8,128)S(1)} %fusion.169, f32[16,8,8192]{2,1,0:T(8,128)} %all-to-all-done, f32[128,128]{1,0:T(8,128)S(1)} %copy-done.5), kind=kOutput, calls=%fused_computation.58 | convolution fusion | flops 340869120 | bytes 25231360 | tf_op jit(solution)/shard_map/dot_general | solution.py:40
  122.4 1.6 copy-done.7
  124.0 0.8 fusion.125
  124.8 16.4 %all-to-all-done.1 = f32[16,8,8192]{2,1,0:T(8,128)} async-done(((f32[16,8,8192]{2,1,0:T(8,128)}), f32[16,8,8192]{2,1,0:T(8,128)}, u32[]{:S(2)}, u32[]{:S(2)}) %all-to-all-start.1) | async-done | bytes 4194336 | tf_op jit(solution)/shard_map/all_to_all | solution.py:95
  141.2 56.6 %all-reduce.6.cloned.1.call-done = f32[128,128]{1,0:T(8,128)} async-done(((f32[128,128]{1,0:T(8,128)}), f32[128,128]{1,0:T(8,128)}) %all-reduce.6.cloned.1.call-update) | async-done | bytes 65552 | tf_op jit(solution)/shard_map/psum | solution.py:15
  197.8 3.1 fusion.171
  200.9 2.9 fusion.67
  203.8 3.1 fusion.173
  207.0 0.3 copy-done.8
  207.3 10.9 %fusion.25 = f32[128,8192]{1,0:T(8,128)} fusion(f32[128,8192]{1,0:T(8,128)S(1)} %copy-done.8, f32[128,8192]{1,0:T(8,128)S(1)} %fusion.171, f32[128,8192]{1,0:T(8,128)S(1)} %fusion.67, f32[128,8192]{1,0:T(8,128)S(1)} %fusion.173, f32[16,8,8192]{2,1,0:T(8,128)} %all-to-all-done.1, f32[128,128]{1,0:T(8,128)S(1)} %copy-done.6), kind=kOutput, calls=%fused_computation.100 | convolution fusion | flops 330383360 | bytes 25231360 | tf_op jit(solution)/shard_map/dot_general | solution.py:40
  218.1 9.7 %scatter_custom_fusion = f32[256,8192]{1,0:T(8,128)} fusion(s32[128]{0:T(128)S(1)} %compare_select_fusion.127, f32[128,8192]{1,0:T(8,128)} %fusion.25, f32[]{:T(128)} %constant.215.clone.1, f32[]{:T(128)} %constant.231.clone.1, f32[]{:T(128)} %constant.230.clone.1, f32[]{:T(128)} %constant.229.clone.1), kind=kCustom, calls=%fused_computation.101 | custom fusion | flops 10485760 | bytes 12585472 | tf_op jit(solution)/shard_map/scatter | solution.py:63
  227.8 23.7 %all-to-all-start.2 = ((f32[16,16,8192]{2,1,0:T(8,128)}), f32[16,16,8192]{2,1,0:T(8,128)}, u32[]{:S(2)}, u32[]{:S(2)}) async-start(f32[16,16,8192]{2,1,0:T(8,128)} %bitcast.73), calls=%async_computation.2 | async-start | bytes 16777216 | tf_op jit(solution)/shard_map/all_to_all | solution.py:65
  251.8 130.7 %all-to-all-done.2 = f32[16,16,8192]{2,1,0:T(8,128)} async-done(((f32[16,16,8192]{2,1,0:T(8,128)}), f32[16,16,8192]{2,1,0:T(8,128)}, u32[]{:S(2)}, u32[]{:S(2)}) %all-to-all-start.2) | async-done | bytes 8388640 | tf_op jit(solution)/shard_map/all_to_all | solution.py:65
  382.5 1.1 subtract_convert_fusion.3
  383.9 0.2 fusion.107
  384.1 0.2 fusion.100
  384.3 0.2 fusion.111
  384.5 0.2 fusion.104
  384.7 0.2 fusion.97
  384.9 0.2 fusion.91
  385.4 0.2 fusion.102
  385.6 0.2 fusion.109
  386.0 0.2 convolution_add_fusion.6
  386.2 0.2 convolution_add_fusion.7
  386.4 0.2 convolution_add_fusion.8
  386.6 0.2 convolution_add_fusion.9
  386.9 4.5 fusion.88
  391.5 0.5 all-gather.2.cloned.1.call-update
  392.0 71.9 %all-reduce.8.cloned.1.call-done = f32[256,512]{1,0:T(8,128)} async-done(((f32[256,512]{1,0:T(8,128)}), f32[256,512]{1,0:T(8,128)}) %all-reduce.8.cloned.1.call-update) | async-done | bytes 524304 | tf_op jit(solution)/shard_map/psum | solution.py:15
  463.9 1.1 subtract_convert_fusion.2
  465.0 48.9 %all-gather.2.cloned.1.call-done = f32[512,8192]{1,0:T(8,128)} async-done(((f32[32,8192]{1,0:T(8,128)}), f32[512,8192]{1,0:T(8,128)}) %all-gather.2.cloned.1.call-update) | async-done | bytes 16777232 | tf_op jit(solution)/shard_map/all_gather | solution.py:71
  513.9 7.6 %subtract_convert_fusion = (bf16[512,8192]{1,0:T(8,128)(2,1)S(1)}, bf16[512,8192]{1,0:T(8,128)(2,1)S(1)}) fusion(f32[512,8192]{1,0:T(8,128)} %all-gather.2.cloned.1.call-done), kind=kLoop, calls=%fused_computation.43 | loop fusion | flops 25165824 | bytes 33554432 | tf_op jit(solution)/shard_map/convert_element_type | solution.py:27
  521.6 4.5 fusion.62
  526.0 4.5 fusion.55
  530.5 4.5 fusion.48
  535.0 4.5 fusion.59
  539.5 4.5 fusion.52
  543.9 4.5 fusion.45
  548.4 4.6 fusion.39
  553.0 4.5 fusion.43
  557.5 4.6 fusion.50
  562.1 1.4 fusion.57
  563.5 1.2 fusion.64
  564.7 8.0 %convolution_add_fusion = f32[256,8192]{1,0:T(8,128)} fusion(f32[256,8192]{1,0:T(8,128)} %fusion.43, bf16[512,8192]{1,0:T(8,128)(2,1)S(1)} %get-tuple-element.6, bf16[256,512]{1,0:T(8,128)(2,1)S(1)} %get-tuple-element.11), kind=kOutput, calls=%fused_computation.70 | convolution fusion | flops 538968064 | bytes 18939904 | tf_op jit(solution)/shard_map/dot_general | solution.py:40
  572.8 8.1 %convolution_add_fusion.1 = f32[256,8192]{1,0:T(8,128)} fusion(f32[256,8192]{1,0:T(8,128)} %fusion.50, bf16[512,8192]{1,0:T(8,128)(2,1)S(1)} %get-tuple-element.6, bf16[256,512]{1,0:T(8,128)(2,1)S(1)} %get-tuple-element.11), kind=kOutput, calls=%fused_computation.71 | convolution fusion | flops 538968064 | bytes 18939904 | tf_op jit(solution)/shard_map/dot_general | solution.py:40
  580.9 4.5 convolution_add_fusion.2
  585.4 5.4 convolution_add_fusion.3
  590.8 0.8 copy-done
  591.6 68.0 %fusion.17 = f32[256,8192]{1,0:T(8,128)} fusion(f32[256,8192]{1,0:T(8,128)} %bitcast.11, f32[256,8192]{1,0:T(8,128)} %fusion.39, f32[256,8192]{1,0:T(8,128)} %convolution_add_fusion, f32[256,8192]{1,0:T(8,128)} %fusion.48, f32[256,8192]{1,0:T(8,128)} %fusion.45, f32[256,8192]{1,0:T(8,128)S(1)} %copy-done, f32[256,8192]{1,0:T(8,128)} %fusion.55, ...), kind=kOutput, calls=%fused_computation.92 | convolution fusion | flops 1021313024 | bytes 111214592 | tf_op jit(solution)/shard_map/dot_general | solution.py:43
  (42 shorter events, 2.4 us)
Async XLA Ops:
  10.8 9.3 %copy-start.10 = (s32[2]{0:T(128)S(1)}, s32[2]{0:T(128)}, u32[]{:S(2)}) copy-start(s32[2]{0:T(128)} %param.10) | copy-start | bytes 28
  10.8 12.5 %copy-start.11 = (s32[1,64]{1,0:T(1,128)S(1)}, s32[1,64]{1,0:T(1,128)}, u32[]{:S(2)}) copy-start(s32[1,64]{1,0:T(1,128)} %param.9) | copy-start | bytes 772
  10.8 62.8 %all-to-all-start = ((f32[16,8,8192]{2,1,0:T(8,128)}), f32[16,8,8192]{2,1,0:T(8,128)}, u32[]{:S(2)}, u32[]{:S(2)}) async-start(f32[16,8,8192]{2,1,0:T(8,128)} %stack.6), calls=%async_computation | async-start | bytes 8388608 | tf_op jit(solution)/shard_map/all_to_all | solution.py:95
  20.1 81.0 %all-reduce.4.cloned.1.call-start = ((), (), s32[]{:S(2)}) async-start(), calls=%async_computation.3 | async-start | bytes 131072 | tf_op jit(solution)/shard_map/psum | solution.py:15
  23.5 2.6 copy-start.3
  23.5 8.1 %copy-start.9 = (s32[128]{0:T(128)S(1)}, s32[128]{0:T(128)}, u32[]{:S(2)}) copy-start(s32[128]{0:T(128)} %param.13) | copy-start | bytes 1540
  26.1 2.0 copy-start.1
  76.0 65.2 %all-to-all-start.1 = ((f32[16,8,8192]{2,1,0:T(8,128)}), f32[16,8,8192]{2,1,0:T(8,128)}, u32[]{:S(2)}, u32[]{:S(2)}) async-start(f32[16,8,8192]{2,1,0:T(8,128)} %stack.7), calls=%async_computation.1 | async-start | bytes 8388608 | tf_op jit(solution)/shard_map/all_to_all | solution.py:95
  88.6 109.3 %all-reduce.6.cloned.1.call-start = ((), (), s32[]{:S(2)}) async-start(), calls=%async_computation.4 | async-start | bytes 131072 | tf_op jit(solution)/shard_map/psum | solution.py:15
  101.1 3.1 copy-start.5
  107.1 3.5 copy-start.2
  121.9 2.0 copy-start.7
  197.8 3.1 copy-start.6
  203.8 3.5 copy-start.8
  227.8 23.8 %copy-start.4 = (f32[512,512]{1,0:T(8,128)S(1)}, f32[512,512]{1,0:T(8,128)}, u32[]{:S(2)}) copy-start(f32[512,512]{1,0:T(8,128)} %param.15) | copy-start | bytes 3145732
  227.8 154.7 %all-to-all-start.2 = ((f32[16,16,8192]{2,1,0:T(8,128)}), f32[16,16,8192]{2,1,0:T(8,128)}, u32[]{:S(2)}, u32[]{:S(2)}) async-start(f32[16,16,8192]{2,1,0:T(8,128)} %bitcast.73), calls=%async_computation.2 | async-start | bytes 16777216 | tf_op jit(solution)/shard_map/all_to_all | solution.py:65
  251.6 212.3 %all-reduce.8.cloned.1.call-start = ((), (), s32[]{:S(2)}) async-start(), calls=%async_computation.5 | async-start | bytes 1048576 | tf_op jit(solution)/shard_map/psum | solution.py:15
  391.4 122.5 %all-gather.2.cloned.1.call-start = ((), (), s32[]{:S(2)}) async-start(), calls=%async_computation.6 | async-start | bytes 17825792 | tf_op jit(solution)/shard_map/all_gather | solution.py:71
  585.4 6.2 copy-start
Sparse Core Ops, SparseCore 0:
  29.1 71.9 all-reduce.3
  125.0 72.8 all-reduce.5
  391.5 72.2 all-reduce.7
Sparse Core Ops, SparseCore 1:
  394.3 119.5 all-gather.1
